TPU v7x, 256 devices: a whole 4x4x8 slice. The times are simulated.
256 devices in a mesh: section: 2 (over core), req: 16 (over x, y), head: 8 (over z).
Axes of the slice: x: 4, y: 4, z: 8, core: 2. Of those that a mesh axis runs over, the one named last changes fastest.
Arguments:
- tokens: bfloat16 [256, 8192], P(None, 'req'), may hold values from -14 to 14
- attention_gain: bfloat16 [2, 8192], P('section', 'req'), may hold values from 0.099609375 to 1.8984375
- query_key_value_weight: bfloat16 [2, 8192, 8, 1280], P('section', 'req', 'head'), may hold values from -0.0625 to 0.0625
- head_output_weight: bfloat16 [2, 8, 1024, 8192], P('section', 'head', None, 'req'), may hold values from -0.0625 to 0.0625
- feedforward_gain: bfloat16 [2, 8192], P('section', 'req'), may hold values from 0.099609375 to 1.8984375
- gate_up: bfloat16 [2, 8192, 2, 14336], P('section', 'req', None, 'head'), may hold values from -0.0625 to 0.0625
- down_weight: bfloat16 [2, 14336, 8192], P('section', 'head', 'req'), may hold values from -0.046875 to 0.046875
- packed_cache: bfloat16 [2, 32768, 8, 256], P('section', 'req', 'head'), may hold values from -70 to 70
- long_cache: bfloat16 [2, 2, 32768, 8, 256], P('section', None, 'req', 'head'), may hold values from -70 to 70
- lengths: int32 [16, 16], P('req'), may hold values from 1 to 256, 2048 in all within a row
- long_split: int32 [2, 16], P(None, 'req'), may hold values from 1 to 2048, 16384 in all within a row
Outputs:
- layer_outputs: bfloat16 [2, 256, 8192], P('section', None, 'req')
Inputs may be any that keep to these rules, and one draw needn't show every extreme that they name: Row g holds the lengths of the 16 requests of request group g in order; they sum to 2048, and the requests' keys fill that group's 2048 slots of packed_cache one request after another. `long_split`: entry (j, g) counts the live slots, the first ones, of group g's 2048 slots of long request j; each row sums to 16384.
All inputs are finite; a program needn't handle non-finite values.
Results may differ from a plain program's by a relative error of at most 0.04.
Values may be sent and summed in bfloat16 or wider, within the bound.
A program may use at most 64 MiB of HBM per device.

v0:
```python
import math
import jax
import jax.numpy as jnp
from jax import lax
from jax.sharding import PartitionSpec as P

MODEL_WIDTH = 8192
QUERY_HEADS = 64
KEY_VALUE_HEADS = 8
HEAD_SIZE = 128
LONG = 16384
EPSILON = 1e-05


def merged(part, axis, combine):
    gathered = jax.tree.map(lambda a: lax.all_gather(a, axis), part)

    def take(source):
        return jax.tree.map(lambda a: lax.dynamic_index_in_dim(a, source, 0, False), gathered)

    return lax.fori_loop(
        1, lax.axis_size(axis), lambda source, state: combine(state, take(source)), take(0)
    )


def shifted(value, axis, by):
    peers = lax.axis_size(axis)
    pairs = [(i, i + by) for i in range(peers) if 0 <= i + by < peers]
    return lax.ppermute(value, axis, pairs)


def rotate(values, position):
    half_dim = values.shape[-1] // 2
    freq_ids = jnp.arange(half_dim).astype(jnp.float32)
    inverse = 1.0 / 10000.0 ** (freq_ids * 2.0 / values.shape[-1])
    angles = position.astype(jnp.float32)[:, None] * inverse[None, :]
    cosine = jnp.cos(angles)[:, None, None, :]
    sine_part = jnp.sin(angles)[:, None, None, :]
    lower_half = values[..., :half_dim]
    upper_half = values[..., half_dim:]
    return jnp.concatenate(
        [
            lower_half * cosine - upper_half * sine_part,
            upper_half * cosine + lower_half * sine_part,
        ],
        -1,
    )


def add_pair(earlier, second_part):
    return earlier + second_part


def combine_partial(earlier, second_part):
    peak = jnp.maximum(earlier[0], second_part[0])
    left_factor = jnp.exp(earlier[0] - peak)
    right_factor = jnp.exp(second_part[0] - peak)
    softmax_total = earlier[1] * left_factor + second_part[1] * right_factor
    weighted_sum = earlier[2] * left_factor[..., None] + second_part[2] * right_factor[..., None]
    return (peak, softmax_total, weighted_sum)


def over_requests(values, combiner):
    return merged(values, "req", combiner)


def rows_apply(values, row_fn):
    return row_fn(lax.all_gather(values, "req", axis=0, tiled=True), jnp.int32(0))


def rows_project(term_fn, row_count):
    return lax.psum_scatter(
        term_fn(jnp.int32(0), row_count * lax.axis_size("req")),
        "req",
        scatter_dimension=0,
        tiled=True,
    )


def head_total(values):
    return lax.psum(values, "head")


def keep_rows(piece_rows, start_row):
    return piece_rows


def norm_rows(values, gain_row):
    floats = values.astype(jnp.float32)
    squares = over_requests(jnp.sum(floats * floats, axis=-1), add_pair)
    return (
        floats * lax.rsqrt(squares / MODEL_WIDTH + EPSILON)[:, None] * gain_row.astype(jnp.float32)
    ).astype(jnp.bfloat16)


def decoder_layer(
    inputs,
    micro_batch,
    attention_gain,
    query_key_value_weight,
    head_output_weight,
    feedforward_gain,
    gate_up,
    down_weight,
    packed_cache,
    long_cache,
    lengths,
    long_split,
):
    req_count = lax.axis_size("req")
    group_index = lax.axis_index("req")
    blocks = inputs.shape[0] // req_count
    columns = query_key_value_weight.shape[1]
    kv_local = query_key_value_weight.shape[2]
    requests_per_group = QUERY_HEADS // KEY_VALUE_HEADS
    score_scale = 1.0 / math.sqrt(HEAD_SIZE)
    normalized_input = norm_rows(inputs, attention_gain[0])
    in_weights = query_key_value_weight[0].reshape(
        columns, kv_local * (requests_per_group + 2) * HEAD_SIZE
    )

    def qkv_term(start_row, row_count):
        return jnp.dot(normalized_input, in_weights, preferred_element_type=jnp.float32)

    projected_rows = rows_project(qkv_term, blocks).reshape(
        blocks, kv_local, requests_per_group + 2, HEAD_SIZE
    )
    local_rows = jnp.arange(blocks)
    row_lengths = lengths[0]
    owner_long = (group_index == 0) | (group_index == req_count // 2)
    long_row = (local_rows == 0) & (micro_batch == 0) & owner_long
    position = row_lengths + jnp.where(long_row, LONG, 0).astype(jnp.int32)
    queries = rotate(projected_rows[:, :, :requests_per_group], position).astype(jnp.bfloat16)
    new_key = rotate(projected_rows[:, :, requests_per_group : requests_per_group + 1], position)[
        :, :, 0
    ].astype(jnp.bfloat16)
    new_value = projected_rows[:, :, requests_per_group + 1].astype(jnp.bfloat16)
    gathered = rows_apply(
        queries[0:1].reshape(1, kv_local * requests_per_group * HEAD_SIZE), keep_rows
    )
    long_queries = jnp.stack([gathered[0], gathered[req_count // 2]]).reshape(
        2, kv_local, requests_per_group, HEAD_SIZE
    )
    far_cache = long_cache[0]
    far_live = (jnp.arange(far_cache.shape[1])[None, :] < long_split[:, 0][:, None])[
        :, None, None, :
    ]
    far_scores = (
        jnp.einsum(
            "jkhd,jpkd->jkhp",
            long_queries,
            far_cache[..., :HEAD_SIZE],
            preferred_element_type=jnp.float32,
        )
        * score_scale
    )
    far_max = jnp.max(jnp.where(far_live, far_scores, -jnp.inf), axis=-1)
    far_weights = jnp.where(
        far_live, jnp.exp(jnp.where(far_live, far_scores - far_max[..., None], 0.0)), 0.0
    ).astype(jnp.bfloat16)
    far_totals = jnp.sum(far_weights.astype(jnp.float32), axis=-1)
    far_summed = jnp.einsum(
        "jkhp,jpkd->jkhd",
        far_weights,
        far_cache[..., HEAD_SIZE:],
        preferred_element_type=jnp.float32,
    )
    far_max, far_totals, far_summed = over_requests(
        (far_max, far_totals, far_summed), combine_partial
    )
    far_index = jnp.where(group_index == 0, 0, 1)
    chosen_max = lax.dynamic_index_in_dim(far_max, far_index, 0, keepdims=False)
    chosen_totals = lax.dynamic_index_in_dim(far_totals, far_index, 0, keepdims=False)
    chosen_summed = lax.dynamic_index_in_dim(far_summed, far_index, 0, keepdims=False)
    pack_part = packed_cache[0]
    seg_ends = jnp.cumsum(lengths[0])
    slot_ids = jnp.arange(pack_part.shape[0])
    slot_owner = jnp.sum((slot_ids[:, None] >= seg_ends[None, :]).astype(jnp.int32), axis=1)
    request_ids = micro_batch * blocks + local_rows
    in_segment = (slot_owner[None, :] == request_ids[:, None])[:, None, None, :]
    scores = (
        jnp.einsum(
            "rkhd,pkd->rkhp",
            queries,
            pack_part[..., :HEAD_SIZE],
            preferred_element_type=jnp.float32,
        )
        * score_scale
    )
    own_score = (
        jnp.einsum("rkhd,rkd->rkh", queries, new_key, preferred_element_type=jnp.float32)
        * score_scale
    )
    row_max = jnp.maximum(jnp.max(jnp.where(in_segment, scores, -jnp.inf), axis=-1), own_score)
    long_mask = long_row[:, None, None]
    row_max = jnp.where(long_mask, jnp.maximum(row_max, chosen_max[None]), row_max)
    weights = jnp.where(
        in_segment, jnp.exp(jnp.where(in_segment, scores - row_max[..., None], 0.0)), 0.0
    ).astype(jnp.bfloat16)
    own_weights = jnp.exp(own_score - row_max).astype(jnp.bfloat16)
    far_factor = jnp.where(
        long_mask, jnp.exp(jnp.where(long_mask, chosen_max[None] - row_max, 0.0)), 0.0
    )
    softmax_total = (
        jnp.sum(weights.astype(jnp.float32), axis=-1)
        + own_weights.astype(jnp.float32)
        + far_factor * chosen_totals[None]
    )
    weighted_sum = jnp.einsum(
        "rkhp,pkd->rkhd", weights, pack_part[..., HEAD_SIZE:], preferred_element_type=jnp.float32
    )
    weighted_sum = (
        weighted_sum
        + own_weights.astype(jnp.float32)[..., None] * new_value.astype(jnp.float32)[:, :, None, :]
    )
    weighted_sum = weighted_sum + far_factor[..., None] * chosen_summed[None]
    attended_heads = (
        (weighted_sum / softmax_total[..., None])
        .astype(jnp.bfloat16)
        .reshape(blocks, kv_local * requests_per_group * HEAD_SIZE)
    )
    out_weights = head_output_weight[0].reshape(kv_local * requests_per_group * HEAD_SIZE, columns)

    def project_heads(piece_rows, start_row):
        return jnp.dot(piece_rows, out_weights, preferred_element_type=jnp.float32)

    attended = head_total(rows_apply(attended_heads, project_heads))
    residual = (inputs.astype(jnp.float32) + attended).astype(jnp.bfloat16)
    normed_two = norm_rows(residual, feedforward_gain[0])
    ff_weights = gate_up[0].reshape(columns, -1)

    def ff_term(start_row, row_count):
        return jnp.dot(normed_two, ff_weights, preferred_element_type=jnp.float32)

    gate_and_up = rows_project(ff_term, blocks)
    hidden_width = gate_and_up.shape[1] // 2
    hidden = (jax.nn.silu(gate_and_up[:, :hidden_width]) * gate_and_up[:, hidden_width:]).astype(
        jnp.bfloat16
    )
    lower_weights = down_weight[0]

    def project_hidden(piece_rows, start_row):
        return jnp.dot(piece_rows, lower_weights, preferred_element_type=jnp.float32)

    lowered = head_total(rows_apply(hidden, project_hidden))
    return (residual.astype(jnp.float32) + lowered).astype(jnp.bfloat16)


def local(
    tokens,
    attention_gain,
    query_key_value_weight,
    head_output_weight,
    feedforward_gain,
    gate_up,
    down_weight,
    packed_cache,
    long_cache,
    lengths,
    long_split,
):
    req_count = lax.axis_size("req")
    section_index = lax.axis_index("section")
    batch_count = 1
    per_group = tokens.shape[0] // req_count
    blocks = per_group // batch_count
    columns = tokens.shape[1]
    token_grid = tokens.reshape(req_count, per_group, columns)
    result = jnp.zeros_like(token_grid)
    incoming = jnp.zeros((req_count * blocks, columns), jnp.bfloat16)
    for phase_step in range(batch_count + 1):
        micro_batch = phase_step - section_index
        is_active = (micro_batch >= 0) & (micro_batch < batch_count)
        micro_batch = jnp.clip(micro_batch, 0, batch_count - 1)
        new_batch = token_grid.reshape(req_count * blocks, columns)
        inputs = jnp.where(section_index == 0, new_batch, incoming)
        output = decoder_layer(
            inputs,
            micro_batch,
            attention_gain,
            query_key_value_weight,
            head_output_weight,
            feedforward_gain,
            gate_up,
            down_weight,
            packed_cache,
            long_cache,
            lengths,
            long_split,
        )
        placed = output.reshape(req_count, blocks, columns)
        result = jnp.where(is_active, placed, result)
        if phase_step < batch_count:
            incoming = shifted(output, "section", 1)
    return result.reshape(1, req_count * per_group, columns)


def solution(mesh):
    placed = (
        P(None, "req"),
        P("section", "req"),
        P("section", "req", "head", None),
        P("section", "head", None, "req"),
        P("section", "req"),
        P("section", "req", None, "head"),
        P("section", "head", "req"),
        P("section", "req", "head", None),
        P("section", None, "req", "head", None),
        P("req", None),
        P(None, "req"),
    )
    return jax.shard_map(
        local, mesh=mesh, in_specs=placed, out_specs=P("section", None, "req"), check_vma=False
    )
```

profile of v0, /device:TPU:2, one launch (start us, length us, event | category | flops | bytes accessed | tf_op | source)
XLA Modules:
  0.0 1032.9 jit_solution(9253363095233518662)
XLA Ops:
  7.8 23.3 %all-gather.10 = f32[16,1,256]{2,1,0:T(1,128)S(1)} all-gather(f32[1,1,256]{2,1,0:T(1,128)S(1)} %bitcast.379), channel_id=2, replica_groups=mesh['section'=2,'req'=16,'head'=8] {'req'}, dimensions={0}, use_global_device_ids=true | all-gather | bytes 17408 | tf_op jit(solution)/shard_map/all_gather | solution.py:16
  36.4 78.1 %reduce-scatter.5.cloned.1.call-done = f32[16,1280]{1,0:T(8,128)} async-done(((f32[256,1280]{1,0:T(8,128)}), f32[16,1280]{1,0:T(8,128)}) %reduce-scatter.5.cloned.1.call-update) | async-done | bytes 81936 | tf_op jit(solution)/shard_map/reduce_scatter | solution.py:72
  115.7 21.4 %all-gather.11 = bf16[16,1,1024]{2,1,0:T(2,128)(2,1)S(1)} all-gather(bf16[1,1,1024]{2,1,0:T(2,128)(2,1)S(1)} %reshape.774), channel_id=1, replica_groups=mesh['section'=2,'req'=16,'head'=8] {'req'}, dimensions={0}, use_global_device_ids=true | all-gather | bytes 34816 | tf_op jit(solution)/shard_map/all_gather | solution.py:68
  140.6 22.6 %all-gather.12 = f32[16,2,8]{2,1,0:T(2,128)S(1)} all-gather(f32[1,2,8]{2,1,0:T(2,128)S(1)} %bitcast.371), channel_id=3, replica_groups=mesh['section'=2,'req'=16,'head'=8] {'req'}, dimensions={0}, use_global_device_ids=true | all-gather | bytes 1088 | tf_op jit(solution)/shard_map/all_gather | solution.py:16
  163.2 21.1 %all-gather.13 = f32[16,2,8]{2,1,0:T(2,128)S(1)} all-gather(f32[1,2,8]{2,1,0:T(2,128)S(1)} %bitcast.375), channel_id=4, replica_groups=mesh['section'=2,'req'=16,'head'=8] {'req'}, dimensions={0}, use_global_device_ids=true | all-gather | bytes 1088 | tf_op jit(solution)/shard_map/all_gather | solution.py:16
  184.3 23.0 %all-gather.3 = f32[32,8,128]{2,1,0:T(8,128)S(1)} all-gather(f32[2,8,128]{2,1,0:T(8,128)S(1)} %fusion.33), channel_id=5, replica_groups=mesh['section'=2,'req'=16,'head'=8] {'req'}, dimensions={0}, use_global_device_ids=true | all-gather | bytes 139264 | tf_op jit(solution)/shard_map/all_gather | solution.py:16
  211.0 21.7 %all_gather.87 = bf16[256,1024]{1,0:T(8,128)(2,1)S(1)} all-gather(bf16[16,1024]{1,0:T(8,128)(2,1)S(1)} %bitcast.340), channel_id=1, replica_groups=mesh['section'=2,'req'=16,'head'=8] {'req'}, dimensions={0}, use_global_device_ids=true | all-gather | bytes 557056 | tf_op jit(solution)/shard_map/all_gather | solution.py:68
  238.6 69.5 %all-reduce.5.cloned.1.call-done = f32[256,512]{1,0:T(8,128)} async-done(((f32[256,512]{1,0:T(8,128)}), f32[256,512]{1,0:T(8,128)}) %all-reduce.5.cloned.1.call-update) | async-done | bytes 524304 | tf_op jit(solution)/shard_map/psum | solution.py:81
  309.3 23.0 %all-gather.14 = f32[16,1,256]{2,1,0:T(1,128)S(1)} all-gather(f32[1,1,256]{2,1,0:T(1,128)S(1)} %bitcast.378), channel_id=6, replica_groups=mesh['section'=2,'req'=16,'head'=8] {'req'}, dimensions={0}, use_global_device_ids=true | all-gather | bytes 17408 | tf_op jit(solution)/shard_map/all_gather | solution.py:16
  338.1 77.9 %reduce-scatter.7.cloned.1.call-done = f32[16,3584]{1,0:T(8,128)} async-done(((f32[256,3584]{1,0:T(8,128)}), f32[16,3584]{1,0:T(8,128)}) %reduce-scatter.7.cloned.1.call-update) | async-done | bytes 229392 | tf_op jit(solution)/shard_map/reduce_scatter | solution.py:72
  417.0 23.0 %all_gather.90 = bf16[256,1792]{1,0:T(8,128)(2,1)S(1)} all-gather(bf16[16,1792]{1,0:T(8,128)(2,1)S(1)} %fusion.70), channel_id=1, replica_groups=mesh['section'=2,'req'=16,'head'=8] {'req'}, dimensions={0}, use_global_device_ids=true | all-gather | bytes 974848 | tf_op jit(solution)/shard_map/all_gather | solution.py:68
  441.6 73.4 %all-reduce.7.cloned.1.call-done = f32[256,512]{1,0:T(8,128)} async-done(((f32[256,512]{1,0:T(8,128)}), f32[256,512]{1,0:T(8,128)}) %all-reduce.7.cloned.1.call-update) | async-done | bytes 524304 | tf_op jit(solution)/shard_map/psum | solution.py:81
  520.5 23.0 %all-gather.15 = f32[16,1,256]{2,1,0:T(1,128)S(1)} all-gather(f32[1,1,256]{2,1,0:T(1,128)S(1)} %bitcast.376), channel_id=7, replica_groups=mesh['section'=2,'req'=16,'head'=8] {'req'}, dimensions={0}, use_global_device_ids=true | all-gather | bytes 17408 | tf_op jit(solution)/shard_map/all_gather | solution.py:16
  546.8 74.6 %reduce-scatter.9.cloned.1.call-done = f32[16,1280]{1,0:T(8,128)} async-done(((f32[256,1280]{1,0:T(8,128)}), f32[16,1280]{1,0:T(8,128)}) %reduce-scatter.9.cloned.1.call-update) | async-done | bytes 81936 | tf_op jit(solution)/shard_map/reduce_scatter | solution.py:72
  622.6 21.5 %all-gather.16 = bf16[16,1,1024]{2,1,0:T(2,128)(2,1)S(1)} all-gather(bf16[1,1,1024]{2,1,0:T(2,128)(2,1)S(1)} %reshape.784), channel_id=1, replica_groups=mesh['section'=2,'req'=16,'head'=8] {'req'}, dimensions={0}, use_global_device_ids=true | all-gather | bytes 34816 | tf_op jit(solution)/shard_map/all_gather | solution.py:68
  649.5 22.6 %all-gather.17 = f32[16,2,8]{2,1,0:T(2,128)S(1)} all-gather(f32[1,2,8]{2,1,0:T(2,128)S(1)} %bitcast.370), channel_id=8, replica_groups=mesh['section'=2,'req'=16,'head'=8] {'req'}, dimensions={0}, use_global_device_ids=true | all-gather | bytes 1088 | tf_op jit(solution)/shard_map/all_gather | solution.py:16
  672.1 21.1 %all-gather.18 = f32[16,2,8]{2,1,0:T(2,128)S(1)} all-gather(f32[1,2,8]{2,1,0:T(2,128)S(1)} %bitcast.374), channel_id=9, replica_groups=mesh['section'=2,'req'=16,'head'=8] {'req'}, dimensions={0}, use_global_device_ids=true | all-gather | bytes 1088 | tf_op jit(solution)/shard_map/all_gather | solution.py:16
  693.2 22.9 %all-gather.8 = f32[32,8,128]{2,1,0:T(8,128)S(1)} all-gather(f32[2,8,128]{2,1,0:T(8,128)S(1)} %fusion.32), channel_id=10, replica_groups=mesh['section'=2,'req'=16,'head'=8] {'req'}, dimensions={0}, use_global_device_ids=true | all-gather | bytes 139264 | tf_op jit(solution)/shard_map/all_gather | solution.py:16
  719.9 22.1 %all_gather.100 = bf16[256,1024]{1,0:T(8,128)(2,1)S(1)} all-gather(bf16[16,1024]{1,0:T(8,128)(2,1)S(1)} %bitcast.341), channel_id=1, replica_groups=mesh['section'=2,'req'=16,'head'=8] {'req'}, dimensions={0}, use_global_device_ids=true | all-gather | bytes 557056 | tf_op jit(solution)/shard_map/all_gather | solution.py:68
  743.4 73.8 %all-reduce.9.cloned.1.call-done = f32[256,512]{1,0:T(8,128)} async-done(((f32[256,512]{1,0:T(8,128)}), f32[256,512]{1,0:T(8,128)}) %all-reduce.9.cloned.1.call-update) | async-done | bytes 524304 | tf_op jit(solution)/shard_map/psum | solution.py:81
  818.4 23.0 %all-gather.19 = f32[16,1,256]{2,1,0:T(1,128)S(1)} all-gather(f32[1,1,256]{2,1,0:T(1,128)S(1)} %bitcast.377), channel_id=11, replica_groups=mesh['section'=2,'req'=16,'head'=8] {'req'}, dimensions={0}, use_global_device_ids=true | all-gather | bytes 17408 | tf_op jit(solution)/shard_map/all_gather | solution.py:16
  847.2 78.0 %reduce-scatter.11.cloned.1.call-done = f32[16,3584]{1,0:T(8,128)} async-done(((f32[256,3584]{1,0:T(8,128)}), f32[16,3584]{1,0:T(8,128)}) %reduce-scatter.11.cloned.1.call-update) | async-done | bytes 229392 | tf_op jit(solution)/shard_map/reduce_scatter | solution.py:72
  926.2 23.0 %all_gather.103 = bf16[256,1792]{1,0:T(8,128)(2,1)S(1)} all-gather(bf16[16,1792]{1,0:T(8,128)(2,1)S(1)} %fusion.69), channel_id=1, replica_groups=mesh['section'=2,'req'=16,'head'=8] {'req'}, dimensions={0}, use_global_device_ids=true | all-gather | bytes 974848 | tf_op jit(solution)/shard_map/all_gather | solution.py:68
  950.7 73.4 %all-reduce.11.cloned.1.call-done = f32[256,512]{1,0:T(8,128)} async-done(((f32[256,512]{1,0:T(8,128)}), f32[256,512]{1,0:T(8,128)}) %all-reduce.11.cloned.1.call-update) | async-done | bytes 524304 | tf_op jit(solution)/shard_map/psum | solution.py:81
  (378 shorter events, 66.3 us)
Async XLA Ops:
  6.5 433.5 %copy-start = (bf16[1,1792,512]{2,1,0:T(8,128)(2,1)S(1)}, bf16[1,1792,512]{2,1,0:T(8,128)(2,1)}, u32[]{:S(2)}) copy-start(bf16[1,1792,512]{2,1,0:T(8,128)(2,1)} %param.29) | copy-start | bytes 5505028
  6.5 108.0 %reduce-scatter.5.cloned.1.call-start = ((), (), s32[]{:S(2)}) async-start(), calls=%async_computation.4 | async-start | bytes 1392640 | tf_op jit(solution)/shard_map/reduce_scatter | solution.py:72
  32.5 3.2 copy-start.9
  32.5 3.7 copy-start.10
  35.6 272.5 %all-reduce.5.cloned.1.call-start = ((), (), s32[]{:S(2)}) async-start(), calls=%async_computation.5 | async-start | bytes 1048576 | tf_op jit(solution)/shard_map/psum | solution.py:81
  35.9 173.5 %copy-start.7 = (bf16[1,2048,1,256]{3,1,2,0:T(8,128)(2,1)S(1)}, bf16[1,2048,1,256]{3,1,2,0:T(8,128)(2,1)}, u32[]{:S(2)}) copy-start(bf16[1,2048,1,256]{3,1,2,0:T(8,128)(2,1)} %param.30) | copy-start | bytes 3145732
  210.1 22.7 %copy-start.3 = (bf16[1,1,1024,512]{3,2,1,0:T(8,128)(2,1)S(1)}, bf16[1,1,1024,512]{3,2,1,0:T(8,128)(2,1)}, u32[]{:S(2)}) copy-start(bf16[1,1,1024,512]{3,2,1,0:T(8,128)(2,1)} %param.26) | copy-start | bytes 3145732
  234.0 182.0 %reduce-scatter.7.cloned.1.call-start = ((), (), s32[]{:S(2)}) async-start(), calls=%async_computation.6 | async-start | bytes 3899392 | tf_op jit(solution)/shard_map/reduce_scatter | solution.py:72
  234.1 4.5 copy-start.8
  234.1 74.0 %copy-start.2 = (bf16[256,512]{1,0:T(8,128)(2,1)S(1)}, bf16[256,512]{1,0:T(8,128)(2,1)}, u32[]{:S(2)}) copy-start(bf16[256,512]{1,0:T(8,128)(2,1)} %param.23) | copy-start | bytes 786436
  309.3 28.8 %copy-start.5 = (bf16[256,512]{1,0:T(8,128)(2,1)}, bf16[256,512]{1,0:T(8,128)(2,1)S(1)}, u32[]{:S(2)}) copy-start(bf16[256,512]{1,0:T(8,128)(2,1)S(1)} %get-tuple-element.859) | copy-start | bytes 786436
  338.1 176.9 %all-reduce.7.cloned.1.call-start = ((), (), s32[]{:S(2)}) async-start(), calls=%async_computation.7 | async-start | bytes 1048576 | tf_op jit(solution)/shard_map/psum | solution.py:81
  441.5 102.7 %copy-start.1 = (bf16[1,512,1,1280]{3,1,2,0:T(8,128)(2,1)S(1)}, bf16[1,512,1,1280]{3,1,2,0:T(8,128)(2,1)}, u32[]{:S(2)}) copy-start(bf16[1,512,1,1280]{3,1,2,0:T(8,128)(2,1)} %param.25) | copy-start | bytes 3932164
  441.5 179.9 %reduce-scatter.9.cloned.1.call-start = ((), (), s32[]{:S(2)}) async-start(), calls=%async_computation.8 | async-start | bytes 1392640 | tf_op jit(solution)/shard_map/reduce_scatter | solution.py:72
  516.9 2.8 collective-permute-start
  546.8 270.4 %all-reduce.9.cloned.1.call-start = ((), (), s32[]{:S(2)}) async-start(), calls=%async_computation.9 | async-start | bytes 1048576 | tf_op jit(solution)/shard_map/psum | solution.py:81
  717.9 24.1 %copy-start.4 = (bf16[1,1,1024,512]{3,2,1,0:T(8,128)(2,1)S(1)}, bf16[1,1,1024,512]{3,2,1,0:T(8,128)(2,1)}, u32[]{:S(2)}) copy-start(bf16[1,1,1024,512]{3,2,1,0:T(8,128)(2,1)} %param.26) | copy-start | bytes 3145732
  719.9 97.2 %copy-start.6 = (bf16[256,512]{1,0:T(8,128)(2,1)S(1)}, bf16[256,512]{1,0:T(8,128)(2,1)}, u32[]{:S(2)}) copy-start(bf16[256,512]{1,0:T(8,128)(2,1)} %get-tuple-element.857) | copy-start | bytes 786436
  743.3 181.8 %reduce-scatter.11.cloned.1.call-start = ((), (), s32[]{:S(2)}) async-start(), calls=%async_computation.10 | async-start | bytes 3899392 | tf_op jit(solution)/shard_map/reduce_scatter | solution.py:72
  847.2 176.9 %all-reduce.11.cloned.1.call-start = ((), (), s32[]{:S(2)}) async-start(), calls=%async_computation.11 | async-start | bytes 1048576 | tf_op jit(solution)/shard_map/psum | solution.py:81
Sparse Core Ops, SparseCore 0:
  35.7 78.7 reduce-scatter.4
  234.1 73.8 all-reduce.4
  338.2 77.7 reduce-scatter.6
  441.6 73.2 all-reduce.6
  546.9 74.4 reduce-scatter.8
  743.4 73.6 all-reduce.8
  847.3 77.8 reduce-scatter.10
  950.8 73.2 all-reduce.10
where the time goes:
time: 1030 us
  waiting for transfers between devices  600 us (58%)
  blocking collectives  358 us (35%)
  matrix products  31.8 us (3%)
  other arithmetic  17.6 us (2%)
  between operations  13.9 us (1%)
    reduce_scatter x4, waiting for transfers between devices, rows_project(): lax.psum_scatter(term_fn(jnp.int32(0), row_count * lax.axis_size('req')),...  309 us
    psum x4, waiting for transfers between devices, head_total(): return lax.psum(values, 'head')  290 us
    all_gather x10, blocking collectives, merged(): gathered = jax.tree.map(lambda a: lax.all_gather(a, axis), part)  226 us
    all_gather x6, blocking collectives, rows_apply(): lax.all_gather(values, 'req', axis=0, tiled=True)  133 us
  transfers between devices with their start and end apart: 9, of which 9 were waited for; matrix products, arithmetic and copies ran while one was open for 1% of the time, Pallas kernels for 0%

commit v1 on v0

--- a/solution.py
+++ b/solution.py
@@ -10,6 +10,7 @@
 HEAD_SIZE = 128
 LONG = 16384
 EPSILON = 1e-05
+members_all_hold = lambda array_here: jnp.sum(lax.all_gather(array_here, axis_name="head"), axis=0)
 
 
 def merged(part, axis, combine):
@@ -78,7 +79,7 @@
 
 
 def head_total(values):
-    return lax.psum(values, "head")
+    return members_all_hold(values)
 
 
 def keep_rows(piece_rows, start_row):

time: 1030 us -> 968 us (0.940)
  waiting for transfers between devices: 600 us -> 526 us
    psum x4 -> x0, waiting for transfers between devices: 290 us -> none  [head_total(): return lax.psum(values, 'head')]
    all_gather x0 -> x4, waiting for transfers between devices: none -> 216 us  [lax.all_gather(array_here, axis_name='head')]
    reduce_sum x0 -> x4, other arithmetic: none -> 11.7 us  [jnp.sum(lax.all_gather(array_here, axis_name='head'), axis=0)]
where the time goes in v1:
time: 968 us; the launch traced here: 967 us
  waiting for transfers between devices  526 us (54%)
  blocking collectives  358 us (37%)
  matrix products  29.8 us (3%)
  other arithmetic  27.3 us (3%)
  between operations  13.9 us (1%)
    reduce_scatter x4, waiting for transfers between devices, rows_project(): lax.psum_scatter(term_fn(jnp.int32(0), row_count * lax.axis_size('req')),...  309 us
    all_gather x10, blocking collectives, merged(): gathered = jax.tree.map(lambda a: lax.all_gather(a, axis), part)  226 us
    all_gather x4, waiting for transfers between devices, lax.all_gather(array_here, axis_name='head')  216 us
    all_gather x6, blocking collectives, rows_apply(): lax.all_gather(values, 'req', axis=0, tiled=True)  132 us
  transfers between devices with their start and end apart: 9, of which 9 were waited for; matrix products, arithmetic and copies ran while one was open for 1% of the time, Pallas kernels for 0%

profile of v1, /device:TPU:2, one launch (start us, length us, event | category | flops | bytes accessed | tf_op | source)
XLA Modules:
  0.0 966.7 jit_solution(17287327241471967967)
XLA Ops:
  7.8 23.3 %all-gather.14 = f32[16,1,256]{2,1,0:T(1,128)S(1)} all-gather(f32[1,1,256]{2,1,0:T(1,128)S(1)} %bitcast.387), channel_id=2, replica_groups=mesh['section'=2,'req'=16,'head'=8] {'req'}, dimensions={0}, use_global_device_ids=true | all-gather | bytes 17408 | tf_op jit(solution)/shard_map/all_gather | solution.py:17
  36.4 78.1 %reduce-scatter.5.cloned.1.call-done = f32[16,1280]{1,0:T(8,128)} async-done(((f32[256,1280]{1,0:T(8,128)}), f32[16,1280]{1,0:T(8,128)}) %reduce-scatter.5.cloned.1.call-update) | async-done | bytes 81936 | tf_op jit(solution)/shard_map/reduce_scatter | solution.py:73
  115.6 21.4 %all-gather.15 = bf16[16,1,1024]{2,1,0:T(2,128)(2,1)S(1)} all-gather(bf16[1,1,1024]{2,1,0:T(2,128)(2,1)S(1)} %reshape.778), channel_id=1, replica_groups=mesh['section'=2,'req'=16,'head'=8] {'req'}, dimensions={0}, use_global_device_ids=true | all-gather | bytes 34816 | tf_op jit(solution)/shard_map/all_gather | solution.py:69
  140.6 23.0 %all-gather.3 = f32[32,8,128]{2,1,0:T(8,128)S(1)} all-gather(f32[2,8,128]{2,1,0:T(8,128)S(1)} %fusion.33), channel_id=5, replica_groups=mesh['section'=2,'req'=16,'head'=8] {'req'}, dimensions={0}, use_global_device_ids=true | all-gather | bytes 139264 | tf_op jit(solution)/shard_map/all_gather | solution.py:17
  163.6 21.1 %all-gather.17 = f32[16,2,8]{2,1,0:T(2,128)S(1)} all-gather(f32[1,2,8]{2,1,0:T(2,128)S(1)} %bitcast.383), channel_id=4, replica_groups=mesh['section'=2,'req'=16,'head'=8] {'req'}, dimensions={0}, use_global_device_ids=true | all-gather | bytes 1088 | tf_op jit(solution)/shard_map/all_gather | solution.py:17
  184.7 22.6 %all-gather.16 = f32[16,2,8]{2,1,0:T(2,128)S(1)} all-gather(f32[1,2,8]{2,1,0:T(2,128)S(1)} %bitcast.379), channel_id=3, replica_groups=mesh['section'=2,'req'=16,'head'=8] {'req'}, dimensions={0}, use_global_device_ids=true | all-gather | bytes 1088 | tf_op jit(solution)/shard_map/all_gather | solution.py:17
  210.9 21.8 %all_gather.111 = bf16[256,1024]{1,0:T(8,128)(2,1)S(1)} all-gather(bf16[16,1024]{1,0:T(8,128)(2,1)S(1)} %bitcast.348), channel_id=1, replica_groups=mesh['section'=2,'req'=16,'head'=8] {'req'}, dimensions={0}, use_global_device_ids=true | all-gather | bytes 557056 | tf_op jit(solution)/shard_map/all_gather | solution.py:69
  238.5 50.8 %all-gather.29.cloned.1.call-done = f32[2048,512]{1,0:T(8,128)} async-done(((f32[256,512]{1,0:T(8,128)}), f32[2048,512]{1,0:T(8,128)}) %all-gather.29.cloned.1.call-update) | async-done | bytes 4194320 | tf_op jit(solution)/shard_map/all_gather | solution.py:13
  292.2 23.0 %all-gather.18 = f32[16,1,256]{2,1,0:T(1,128)S(1)} all-gather(f32[1,1,256]{2,1,0:T(1,128)S(1)} %bitcast.386), channel_id=7, replica_groups=mesh['section'=2,'req'=16,'head'=8] {'req'}, dimensions={0}, use_global_device_ids=true | all-gather | bytes 17408 | tf_op jit(solution)/shard_map/all_gather | solution.py:17
  321.0 78.1 %reduce-scatter.7.cloned.1.call-done = f32[16,3584]{1,0:T(8,128)} async-done(((f32[256,3584]{1,0:T(8,128)}), f32[16,3584]{1,0:T(8,128)}) %reduce-scatter.7.cloned.1.call-update) | async-done | bytes 229392 | tf_op jit(solution)/shard_map/reduce_scatter | solution.py:73
  400.1 23.0 %all_gather.116 = bf16[256,1792]{1,0:T(8,128)(2,1)S(1)} all-gather(bf16[16,1792]{1,0:T(8,128)(2,1)S(1)} %fusion.70), channel_id=1, replica_groups=mesh['section'=2,'req'=16,'head'=8] {'req'}, dimensions={0}, use_global_device_ids=true | all-gather | bytes 974848 | tf_op jit(solution)/shard_map/all_gather | solution.py:69
  424.7 54.8 %all-gather.31.cloned.1.call-done = f32[2048,512]{1,0:T(8,128)} async-done(((f32[256,512]{1,0:T(8,128)}), f32[2048,512]{1,0:T(8,128)}) %all-gather.31.cloned.1.call-update) | async-done | bytes 4194320 | tf_op jit(solution)/shard_map/all_gather | solution.py:13
  489.0 23.0 %all-gather.19 = f32[16,1,256]{2,1,0:T(1,128)S(1)} all-gather(f32[1,1,256]{2,1,0:T(1,128)S(1)} %bitcast.384), channel_id=9, replica_groups=mesh['section'=2,'req'=16,'head'=8] {'req'}, dimensions={0}, use_global_device_ids=true | all-gather | bytes 17408 | tf_op jit(solution)/shard_map/all_gather | solution.py:17
  515.4 74.7 %reduce-scatter.9.cloned.1.call-done = f32[16,1280]{1,0:T(8,128)} async-done(((f32[256,1280]{1,0:T(8,128)}), f32[16,1280]{1,0:T(8,128)}) %reduce-scatter.9.cloned.1.call-update) | async-done | bytes 81936 | tf_op jit(solution)/shard_map/reduce_scatter | solution.py:73
  591.3 21.4 %all-gather.20 = bf16[16,1,1024]{2,1,0:T(2,128)(2,1)S(1)} all-gather(bf16[1,1,1024]{2,1,0:T(2,128)(2,1)S(1)} %reshape.788), channel_id=1, replica_groups=mesh['section'=2,'req'=16,'head'=8] {'req'}, dimensions={0}, use_global_device_ids=true | all-gather | bytes 34816 | tf_op jit(solution)/shard_map/all_gather | solution.py:69
  616.3 23.0 %all-gather.10 = f32[32,8,128]{2,1,0:T(8,128)S(1)} all-gather(f32[2,8,128]{2,1,0:T(8,128)S(1)} %fusion.32), channel_id=12, replica_groups=mesh['section'=2,'req'=16,'head'=8] {'req'}, dimensions={0}, use_global_device_ids=true | all-gather | bytes 139264 | tf_op jit(solution)/shard_map/all_gather | solution.py:17
  639.2 21.1 %all-gather.22 = f32[16,2,8]{2,1,0:T(2,128)S(1)} all-gather(f32[1,2,8]{2,1,0:T(2,128)S(1)} %bitcast.382), channel_id=11, replica_groups=mesh['section'=2,'req'=16,'head'=8] {'req'}, dimensions={0}, use_global_device_ids=true | all-gather | bytes 1088 | tf_op jit(solution)/shard_map/all_gather | solution.py:17
  660.3 22.8 %all-gather.21 = f32[16,2,8]{2,1,0:T(2,128)S(1)} all-gather(f32[1,2,8]{2,1,0:T(2,128)S(1)} %bitcast.378), channel_id=10, replica_groups=mesh['section'=2,'req'=16,'head'=8] {'req'}, dimensions={0}, use_global_device_ids=true | all-gather | bytes 1088 | tf_op jit(solution)/shard_map/all_gather | solution.py:17
  686.8 21.8 %all_gather.128 = bf16[256,1024]{1,0:T(8,128)(2,1)S(1)} all-gather(bf16[16,1024]{1,0:T(8,128)(2,1)S(1)} %bitcast.349), channel_id=1, replica_groups=mesh['section'=2,'req'=16,'head'=8] {'req'}, dimensions={0}, use_global_device_ids=true | all-gather | bytes 557056 | tf_op jit(solution)/shard_map/all_gather | solution.py:69
  709.9 55.3 %all-gather.33.cloned.1.call-done = f32[2048,512]{1,0:T(8,128)} async-done(((f32[256,512]{1,0:T(8,128)}), f32[2048,512]{1,0:T(8,128)}) %all-gather.33.cloned.1.call-update) | async-done | bytes 4194320 | tf_op jit(solution)/shard_map/all_gather | solution.py:13
  768.1 23.0 %all-gather.23 = f32[16,1,256]{2,1,0:T(1,128)S(1)} all-gather(f32[1,1,256]{2,1,0:T(1,128)S(1)} %bitcast.385), channel_id=14, replica_groups=mesh['section'=2,'req'=16,'head'=8] {'req'}, dimensions={0}, use_global_device_ids=true | all-gather | bytes 17408 | tf_op jit(solution)/shard_map/all_gather | solution.py:17
  796.9 78.1 %reduce-scatter.11.cloned.1.call-done = f32[16,3584]{1,0:T(8,128)} async-done(((f32[256,3584]{1,0:T(8,128)}), f32[16,3584]{1,0:T(8,128)}) %reduce-scatter.11.cloned.1.call-update) | async-done | bytes 229392 | tf_op jit(solution)/shard_map/reduce_scatter | solution.py:73
  876.0 23.1 %all_gather.133 = bf16[256,1792]{1,0:T(8,128)(2,1)S(1)} all-gather(bf16[16,1792]{1,0:T(8,128)(2,1)S(1)} %fusion.69), channel_id=1, replica_groups=mesh['section'=2,'req'=16,'head'=8] {'req'}, dimensions={0}, use_global_device_ids=true | all-gather | bytes 974848 | tf_op jit(solution)/shard_map/all_gather | solution.py:69
  900.5 54.8 %all-gather.35.cloned.1.call-done = f32[2048,512]{1,0:T(8,128)} async-done(((f32[256,512]{1,0:T(8,128)}), f32[2048,512]{1,0:T(8,128)}) %all-gather.35.cloned.1.call-update) | async-done | bytes 4194320 | tf_op jit(solution)/shard_map/all_gather | solution.py:13
  (384 shorter events, 74.3 us)
Async XLA Ops:
  6.5 416.6 %copy-start = (bf16[1,1792,512]{2,1,0:T(8,128)(2,1)S(1)}, bf16[1,1792,512]{2,1,0:T(8,128)(2,1)}, u32[]{:S(2)}) copy-start(bf16[1,1792,512]{2,1,0:T(8,128)(2,1)} %param.29) | copy-start | bytes 5505028
  6.5 108.0 %reduce-scatter.5.cloned.1.call-start = ((), (), s32[]{:S(2)}) async-start(), calls=%async_computation.4 | async-start | bytes 1392640 | tf_op jit(solution)/shard_map/reduce_scatter | solution.py:73
  32.5 3.2 copy-start.10
  32.5 3.7 copy-start.11
  35.6 253.7 %all-gather.29.cloned.1.call-start = ((), (), s32[]{:S(2)}) async-start(), calls=%async_computation.8 | async-start | bytes 4718592 | tf_op jit(solution)/shard_map/all_gather | solution.py:13
  36.1 173.3 %copy-start.7 = (bf16[1,2048,1,256]{3,1,2,0:T(8,128)(2,1)S(1)}, bf16[1,2048,1,256]{3,1,2,0:T(8,128)(2,1)}, u32[]{:S(2)}) copy-start(bf16[1,2048,1,256]{3,1,2,0:T(8,128)(2,1)} %param.30) | copy-start | bytes 3145732
  209.9 22.7 %copy-start.3 = (bf16[1,1,1024,512]{3,2,1,0:T(8,128)(2,1)S(1)}, bf16[1,1,1024,512]{3,2,1,0:T(8,128)(2,1)}, u32[]{:S(2)}) copy-start(bf16[1,1,1024,512]{3,2,1,0:T(8,128)(2,1)} %param.26) | copy-start | bytes 3145732
  234.0 165.1 %reduce-scatter.7.cloned.1.call-start = ((), (), s32[]{:S(2)}) async-start(), calls=%async_computation.5 | async-start | bytes 3899392 | tf_op jit(solution)/shard_map/reduce_scatter | solution.py:73
  234.0 4.5 copy-start.9
  289.3 2.7 copy-start.2
  292.2 28.7 %copy-start.5 = (bf16[256,512]{1,0:T(8,128)(2,1)}, bf16[256,512]{1,0:T(8,128)(2,1)S(1)}, u32[]{:S(2)}) copy-start(bf16[256,512]{1,0:T(8,128)(2,1)S(1)} %get-tuple-element.859) | copy-start | bytes 786436
  321.0 158.5 %all-gather.31.cloned.1.call-start = ((), (), s32[]{:S(2)}) async-start(), calls=%async_computation.9 | async-start | bytes 4718592 | tf_op jit(solution)/shard_map/all_gather | solution.py:13
  424.6 165.5 %reduce-scatter.9.cloned.1.call-start = ((), (), s32[]{:S(2)}) async-start(), calls=%async_computation.6 | async-start | bytes 1392640 | tf_op jit(solution)/shard_map/reduce_scatter | solution.py:73
  483.0 29.8 %copy-start.1 = (bf16[1,512,1,1280]{3,1,2,0:T(8,128)(2,1)S(1)}, bf16[1,512,1,1280]{3,1,2,0:T(8,128)(2,1)}, u32[]{:S(2)}) copy-start(bf16[1,512,1,1280]{3,1,2,0:T(8,128)(2,1)} %param.25) | copy-start | bytes 3932164
  485.0 3.2 collective-permute-start
  515.4 169.8 %copy-start.8 = (bf16[1,2048,1,256]{3,1,2,0:T(8,128)(2,1)S(1)}, bf16[1,2048,1,256]{3,1,2,0:T(8,128)(2,1)}, u32[]{:S(2)}) copy-start(bf16[1,2048,1,256]{3,1,2,0:T(8,128)(2,1)} %param.30) | copy-start | bytes 3145732
  515.4 249.8 %all-gather.33.cloned.1.call-start = ((), (), s32[]{:S(2)}) async-start(), calls=%async_computation.10 | async-start | bytes 4718592 | tf_op jit(solution)/shard_map/all_gather | solution.py:13
  685.8 22.7 %copy-start.4 = (bf16[1,1,1024,512]{3,2,1,0:T(8,128)(2,1)S(1)}, bf16[1,1,1024,512]{3,2,1,0:T(8,128)(2,1)}, u32[]{:S(2)}) copy-start(bf16[1,1,1024,512]{3,2,1,0:T(8,128)(2,1)} %param.26) | copy-start | bytes 3145732
  709.8 165.1 %reduce-scatter.11.cloned.1.call-start = ((), (), s32[]{:S(2)}) async-start(), calls=%async_computation.7 | async-start | bytes 3899392 | tf_op jit(solution)/shard_map/reduce_scatter | solution.py:73
  765.2 2.7 copy-start.6
  796.8 158.5 %all-gather.35.cloned.1.call-start = ((), (), s32[]{:S(2)}) async-start(), calls=%async_computation.11 | async-start | bytes 4718592 | tf_op jit(solution)/shard_map/all_gather | solution.py:13
Sparse Core Ops, SparseCore 0:
  35.7 78.7 reduce-scatter.4
  234.1 55.1 all-gather.28
  321.1 77.9 reduce-scatter.6
  424.8 54.6 all-gather.30
  515.5 74.6 reduce-scatter.8
  710.0 55.1 all-gather.32
  797.0 77.9 reduce-scatter.10
  900.6 54.6 all-gather.34
